TPU v7x, 32 devices: a whole 2x2x4 slice. The times are simulated.
32 devices in a mesh: groups: 2 (over y), tm: 8 (over z, x), head: 2 (over core).
Axes of the slice: x: 2, y: 2, z: 4, core: 2. Of those that a mesh axis runs over, the one named last changes fastest.
Arguments:
- queries: bfloat16 [1536, 2560], P(('groups', 'tm'), 'head'), parts along dimension 0, may hold values from -1000 to 1000
- keys: bfloat16 [1536, 2560], P(('groups', 'tm'), 'head'), parts along dimension 0, may hold values from -1000 to 1000
- values: bfloat16 [1536, 2560], P(('groups', 'tm'), 'head'), parts along dimension 0, may hold values from -6 to 6
- q_gain: float32 [2560], P('head'), may hold values from 1 to 2
- k_gain: float32 [2560], P('head'), may hold values from 1 to 2
- frames: int32 [16], P(('groups', 'tm')), parts along dimension 0, may hold values from 1 to 3
- flags: int32 [16, 2], P(('groups', 'tm')), parts along dimension 0, may hold values 0 or 1
Outputs:
- attended: bfloat16 [1536, 2560], P(('groups', 'tm'), 'head'), parts along dimension 0
There are 2 independent parts, one for each index of `groups`. A program takes and returns all parts, laid end to end along the dimension named above; an argument that names none is the same for every part. Nothing has to cross between parts.
All inputs are finite; a program needn't handle non-finite values. No bound on the sum of `flags` on one device may be relied on, other than what follows from the above.
Results may differ from a plain program's by a relative error of at most 0.011.
Values may be sent and summed in bfloat16 or wider, within the bound.
No kernel may reach another device: no remote copies, remote signals or barrier semaphores. Data moves between devices by JAX's collectives and lax.ppermute only.
A program may use at most 128 MiB of HBM per device.

v0:
```python
from functools import reduce
import math
import jax
import jax.numpy as jnp
from jax import lax
from jax.sharding import PartitionSpec as P

HD = 128
FT = 32
EPSILON = 1e-06


def passed_along(value, axis, steps):
    count = lax.axis_size(axis)
    first, last = (max(0, -steps), min(count, count - steps))
    return lax.ppermute(value, axis, [(source, source + steps) for source in range(first, last)])


def spread(value, axis, source):
    kept = jnp.where(lax.axis_index(axis) == source, value, 0).astype(value.dtype)
    return lax.psum(kept, axis)


def slide_rows(buffer, offset_rows, window_len):
    filler = jnp.zeros((window_len,) + buffer.shape[1:], buffer.dtype)
    return lax.dynamic_slice_in_dim(
        jnp.concatenate([buffer, filler], 0), offset_rows, window_len, 0
    )


def append_window(earlier, later):
    window_len = later[2].shape[0]
    later_count = jnp.sum(later[2].astype(jnp.float32)).astype(jnp.int32)
    from_later = jnp.arange(window_len, dtype=jnp.int32) >= window_len - later_count
    merged = []
    for previous, incoming in zip(earlier, later):
        shifted = slide_rows(previous, later_count, window_len)
        choose_mask = from_later.reshape((window_len,) + (1,) * (incoming.ndim - 1))
        merged.append(jnp.where(choose_mask, incoming, shifted))
    return tuple(merged)


def local(queries, keys, values, q_gain, k_gain, frames, flags):
    row_count, col_count = queries.shape
    head_count = col_count // HD
    full_width = col_count * lax.axis_size("head")
    q_wide = queries.astype(jnp.float32)
    k_wide = keys.astype(jnp.float32)
    q_energy, k_energy = lax.psum(
        (jnp.sum(q_wide * q_wide, axis=1), jnp.sum(k_wide * k_wide, axis=1)), "head"
    )
    q_norm = (q_wide * lax.rsqrt(q_energy / full_width + EPSILON)[:, None] * q_gain).astype(
        jnp.bfloat16
    )
    k_norm = (k_wide * lax.rsqrt(k_energy / full_width + EPSILON)[:, None] * k_gain).astype(
        jnp.bfloat16
    )
    valid_rows = frames[0] * FT
    window_len = 2 * FT

    def tail_rows(source):
        leading = jnp.zeros((window_len, col_count), jnp.bfloat16)
        return slide_rows(jnp.concatenate([leading, source], 0), valid_rows, window_len)

    own_flags = (jnp.arange(window_len, dtype=jnp.int32) >= window_len - valid_rows).astype(
        jnp.bfloat16
    )
    own_window = (tail_rows(k_norm), tail_rows(values), own_flags)
    from_last = passed_along((own_window[0], own_window[1], own_window[2]), "tm", 1)
    from_earlier = passed_along((own_window[0], own_window[1], own_window[2]), "tm", 2)
    window_keys, window_values, window_flags = append_window(from_earlier, from_last)
    sink_keys, sink_values = (spread(k_norm[:FT], "tm", 0), spread(values[:FT], "tm", 0))
    scaling = 1.0 / math.sqrt(HD)
    q_heads = q_norm.reshape(row_count, head_count, HD)
    slot_index = jnp.arange(row_count, dtype=jnp.int32)
    live_keys = slot_index < valid_rows
    use_sink = flags[0, 0] > 0
    use_window = flags[0, 1] > 0
    key_groups = (
        (k_norm, values, live_keys),
        (window_keys, window_values, (window_flags > 0) & use_window),
        (sink_keys, sink_values, jnp.full((sink_keys.shape[0],), use_sink)),
    )

    def score_block(key_rows, allowed):
        k_heads = key_rows.reshape(key_rows.shape[0], head_count, HD)
        products = (
            jnp.einsum("qhd,khd->hqk", q_heads, k_heads, preferred_element_type=jnp.float32)
            * scaling
        )
        return jnp.where(allowed[None, None, :], products, -jnp.inf)

    logits = [score_block(key_rows, allowed) for key_rows, value_rows, allowed in key_groups]
    highest = reduce(
        jnp.maximum, [jnp.max(block_scores, axis=2, keepdims=True) for block_scores in logits]
    )
    denominator = jnp.zeros((head_count, row_count), jnp.float32)
    blended = jnp.zeros((row_count, head_count, HD), jnp.float32)
    for block_scores, group in zip(logits, key_groups):
        weight = jnp.exp(block_scores - highest).astype(jnp.bfloat16)
        denominator = denominator + jnp.sum(weight, axis=2, dtype=jnp.float32)
        value_heads = group[1].reshape(group[1].shape[0], head_count, HD)
        blended = blended + jnp.einsum(
            "hqk,khd->qhd", weight, value_heads, preferred_element_type=jnp.float32
        )
    blended = blended / jnp.transpose(denominator)[:, :, None]
    blended = jnp.where(live_keys[:, None, None], blended, 0.0)
    return blended.reshape(row_count, col_count).astype(jnp.bfloat16)


def solution(mesh):
    placed = (
        P(("groups", "tm"), "head"),
        P(("groups", "tm"), "head"),
        P(("groups", "tm"), "head"),
        P("head"),
        P("head"),
        P(("groups", "tm")),
        P(("groups", "tm"), None),
    )
    return jax.shard_map(
        local, mesh=mesh, in_specs=placed, out_specs=P(("groups", "tm"), "head"), check_vma=False
    )
```

profile of v0, /device:TPU:0, one launch (start us, length us, event | category | flops | bytes accessed | tf_op | source)
XLA Modules:
  0.0 111.2 jit_solution(5486374469623921674)
XLA Ops:
  7.2 5.0 %collective-permute-start.1 = (bf16[64]{0:T(256)(128)(2,1)S(1)}, bf16[64]{0:T(256)(128)(2,1)S(1)}, u32[]{:S(2)}, u32[]{:S(2)}) collective-permute-start(bf16[64]{0:T(256)(128)(2,1)S(1)} %compare_convert_fusion), channel_id=1, source_target_pairs={{0,4},{2,6},{4,8},{6,10},{8,12},{10,14},{1,5},{3,7},{5,9},{7,11},{... | collective-permute-start | bytes 392 | tf_op jit(solution)/shard_map/ppermute | solution.py:16
  12.2 3.4 %collective-permute-start = (bf16[64]{0:T(256)(128)(2,1)S(1)}, bf16[64]{0:T(256)(128)(2,1)S(1)}, u32[]{:S(2)}, u32[]{:S(2)}) collective-permute-start(bf16[64]{0:T(256)(128)(2,1)S(1)} %compare_convert_fusion), channel_id=1, source_target_pairs={{0,2},{2,4},{4,6},{6,8},{8,10},{10,12},{12,14},{1,3},{3,5},{5,7},{... | collective-permute-start | bytes 392 | tf_op jit(solution)/shard_map/ppermute | solution.py:16
  15.6 1.1 fusion.7
  16.7 0.1 fusion.10
  16.9 2.5 %all-reduce.3 = (f32[96]{0:T(128)S(1)}, f32[96]{0:T(128)S(1)}) all-reduce(f32[96]{0:T(128)S(1)} %fusion.7, f32[96]{0:T(128)S(1)} %fusion.10), channel_id=1, replica_groups=mesh['groups'=2,'tm'=8,'head'=2] {'head'}, use_global_device_ids=true, to_apply=%region_1.0 | all-reduce | flops 192 | bytes 1536 | tf_op jit(solution)/shard_map/psum | solution.py:49
  19.4 0.1 fusion.12
  19.5 0.8 copy-done
  20.3 0.2 fusion.18
  20.5 3.5 %collective-permute-start.4 = (bf16[64,1280]{1,0:T(8,128)(2,1)S(1)}, bf16[64,1280]{1,0:T(8,128)(2,1)S(1)}, u32[]{:S(2)}, u32[]{:S(2)}) collective-permute-start(bf16[64,1280]{1,0:T(8,128)(2,1)S(1)} %get-tuple-element.9), channel_id=1, source_target_pairs={{0,2},{2,4},{4,6},{6,8},{8,10},{10,12},{12,14},{1,3},{3,5},{5,7},{... | collective-permute-start | bytes 491528 | tf_op jit(solution)/shard_map/ppermute | solution.py:16
  24.0 3.5 %collective-permute-start.5 = (bf16[64,1280]{1,0:T(8,128)(2,1)S(1)}, bf16[64,1280]{1,0:T(8,128)(2,1)S(1)}, u32[]{:S(2)}, u32[]{:S(2)}) collective-permute-start(bf16[64,1280]{1,0:T(8,128)(2,1)S(1)} %get-tuple-element.9), channel_id=1, source_target_pairs={{0,4},{2,6},{4,8},{6,10},{8,12},{10,14},{1,5},{3,7},{5,9},{7,11},{... | collective-permute-start | bytes 491528 | tf_op jit(solution)/shard_map/ppermute | solution.py:16
  27.5 3.4 %collective-permute-start.2 = (bf16[64,1280]{1,0:T(8,128)(2,1)S(1)}, bf16[64,1280]{1,0:T(8,128)(2,1)S(1)}, u32[]{:S(2)}, u32[]{:S(2)}) collective-permute-start(bf16[64,1280]{1,0:T(8,128)(2,1)S(1)} %get-tuple-element.10), channel_id=1, source_target_pairs={{0,2},{2,4},{4,6},{6,8},{8,10},{10,12},{12,14},{1,3},{3,5},{5,7},{... | collective-permute-start | bytes 491528 | tf_op jit(solution)/shard_map/ppermute | solution.py:16
  30.9 0.6 copy_bitcast_fusion
  31.5 0.7 copy_bitcast_fusion.1
  32.2 0.2 copy.17
  32.5 0.2 copy.24
  32.7 0.4 copy-done.5
  33.1 0.6 fusion.26
  33.9 0.2 copy.16
  34.7 0.3 fusion.28
  35.7 1.9 %collective-permute-start.3 = (bf16[64,1280]{1,0:T(8,128)(2,1)S(1)}, bf16[64,1280]{1,0:T(8,128)(2,1)S(1)}, u32[]{:S(2)}, u32[]{:S(2)}) collective-permute-start(bf16[64,1280]{1,0:T(8,128)(2,1)S(1)} %get-tuple-element.10), channel_id=1, source_target_pairs={{0,4},{2,6},{4,8},{6,10},{8,12},{10,14},{1,5},{3,7},{5,9},{7,11},{... | collective-permute-start | bytes 491528 | tf_op jit(solution)/shard_map/ppermute | solution.py:16
  37.6 0.7 convert_reduce_fusion.3
  39.0 60.8 %all-reduce.7.cloned.1.call-done = (bf16[32,10,128]{2,0,1:T(8,128)(2,1)}, bf16[32,10,128]{2,0,1:T(8,128)(2,1)}) async-done(((bf16[32,10,128]{2,0,1:T(8,128)(2,1)}, bf16[32,10,128]{2,0,1:T(8,128)(2,1)}), (bf16[32,10,128]{2,0,1:T(8,128)(2,1)}, bf16[32,10,128]{2,0,1:T(8,128)(2,1)})) %all-reduce.7.cloned.1.call-update) | async-done | bytes 163856 | tf_op jit(solution)/shard_map/psum | solution.py:21
  99.8 1.1 fusion.27
  100.9 0.2 fusion.16
  101.1 0.2 select_reduce_fusion
  101.4 0.1 convert_reduce_fusion.1
  101.7 0.4 convolution_bitcast_fusion.2
  102.0 0.4 fusion.1
  102.4 0.5 copy-done.6
  102.9 0.3 fusion.5
  103.3 0.2 copy.29
  103.5 0.9 copy.30
  (30 shorter events, 0.5 us)
Async XLA Ops:
  6.5 10.2 %copy-start.1 = (bf16[96,1280]{1,0:T(8,128)(2,1)S(1)}, bf16[96,1280]{1,0:T(8,128)(2,1)}, u32[]{:S(2)}) copy-start(bf16[96,1280]{1,0:T(8,128)(2,1)} %param.8) | copy-start | bytes 737284
  6.5 93.2 %all-reduce.7.cloned.1.call-start = ((), (), s32[]{:S(2)}) async-start(), calls=%async_computation | async-start | bytes 327680 | tf_op jit(solution)/shard_map/psum | solution.py:21
  7.2 31.7 %collective-permute-start.1 = (bf16[64]{0:T(256)(128)(2,1)S(1)}, bf16[64]{0:T(256)(128)(2,1)S(1)}, u32[]{:S(2)}, u32[]{:S(2)}) collective-permute-start(bf16[64]{0:T(256)(128)(2,1)S(1)} %compare_convert_fusion), channel_id=1, source_target_pairs={{0,4},{2,6},{4,8},{6,10},{8,12},{10,14},{1,5},{3,7},{5,9},{7,11},{... | collective-permute-start | bytes 392 | tf_op jit(solution)/shard_map/ppermute | solution.py:16
  12.2 23.5 %collective-permute-start = (bf16[64]{0:T(256)(128)(2,1)S(1)}, bf16[64]{0:T(256)(128)(2,1)S(1)}, u32[]{:S(2)}, u32[]{:S(2)}) collective-permute-start(bf16[64]{0:T(256)(128)(2,1)S(1)} %compare_convert_fusion), channel_id=1, source_target_pairs={{0,2},{2,4},{4,6},{6,8},{8,10},{10,12},{12,14},{1,3},{3,5},{5,7},{... | collective-permute-start | bytes 392 | tf_op jit(solution)/shard_map/ppermute | solution.py:16
  16.9 2.5 %copy-start.3 = (f32[1280]{0:T(1024)S(1)}, f32[1280]{0:T(1024)}, u32[]{:S(2)}) copy-start(f32[1280]{0:T(1024)} %param.11) | copy-start | bytes 15364
  19.4 0.9 copy-start
  20.5 80.4 %collective-permute-start.4 = (bf16[64,1280]{1,0:T(8,128)(2,1)S(1)}, bf16[64,1280]{1,0:T(8,128)(2,1)S(1)}, u32[]{:S(2)}, u32[]{:S(2)}) collective-permute-start(bf16[64,1280]{1,0:T(8,128)(2,1)S(1)} %get-tuple-element.9), channel_id=1, source_target_pairs={{0,2},{2,4},{4,6},{6,8},{8,10},{10,12},{12,14},{1,3},{3,5},{5,7},{... | collective-permute-start | bytes 491528 | tf_op jit(solution)/shard_map/ppermute | solution.py:16
  24.0 76.9 %collective-permute-start.5 = (bf16[64,1280]{1,0:T(8,128)(2,1)S(1)}, bf16[64,1280]{1,0:T(8,128)(2,1)S(1)}, u32[]{:S(2)}, u32[]{:S(2)}) collective-permute-start(bf16[64,1280]{1,0:T(8,128)(2,1)S(1)} %get-tuple-element.9), channel_id=1, source_target_pairs={{0,4},{2,6},{4,8},{6,10},{8,12},{10,14},{1,5},{3,7},{5,9},{7,11},{... | collective-permute-start | bytes 491528 | tf_op jit(solution)/shard_map/ppermute | solution.py:16
  27.5 73.4 %collective-permute-start.2 = (bf16[64,1280]{1,0:T(8,128)(2,1)S(1)}, bf16[64,1280]{1,0:T(8,128)(2,1)S(1)}, u32[]{:S(2)}, u32[]{:S(2)}) collective-permute-start(bf16[64,1280]{1,0:T(8,128)(2,1)S(1)} %get-tuple-element.10), channel_id=1, source_target_pairs={{0,2},{2,4},{4,6},{6,8},{8,10},{10,12},{12,14},{1,3},{3,5},{5,7},{... | collective-permute-start | bytes 491528 | tf_op jit(solution)/shard_map/ppermute | solution.py:16
  32.4 0.7 copy-start.5
  32.4 1.3 %copy-start.2 = (bf16[96,1280]{1,0:T(8,128)(2,1)S(1)}, bf16[96,1280]{1,0:T(8,128)(2,1)}, u32[]{:S(2)}) copy-start(bf16[96,1280]{1,0:T(8,128)(2,1)} %param.7) | copy-start | bytes 737284
  32.5 1.3 %copy-start.4 = (f32[1280]{0:T(1024)S(1)}, f32[1280]{0:T(1024)}, u32[]{:S(2)}) copy-start(f32[1280]{0:T(1024)} %param.10) | copy-start | bytes 15364
  35.7 65.2 %collective-permute-start.3 = (bf16[64,1280]{1,0:T(8,128)(2,1)S(1)}, bf16[64,1280]{1,0:T(8,128)(2,1)S(1)}, u32[]{:S(2)}, u32[]{:S(2)}) collective-permute-start(bf16[64,1280]{1,0:T(8,128)(2,1)S(1)} %get-tuple-element.10), channel_id=1, source_target_pairs={{0,4},{2,6},{4,8},{6,10},{8,12},{10,14},{1,5},{3,7},{5,9},{7,11},{... | collective-permute-start | bytes 491528 | tf_op jit(solution)/shard_map/ppermute | solution.py:16
  102.0 0.9 copy-start.6
Sparse Core Ops, SparseCore 0:
  32.3 67.4 all-reduce.6
where the time goes:
time: 112 us; the launch traced here: 111 us
  waiting for transfers between devices  60.8 us (54%)
  starting transfers between devices  20.6 us (18%)
  between operations  16.3 us (15%)
  other arithmetic  4.21 us (4%)
  local copies, waits for them, and re-layouts  4.14 us (4%)
  matrix products  2.67 us (2%)
  blocking collectives  2.47 us (2%)
    psum x1, waiting for transfers between devices, spread(): return lax.psum(kept, axis)  60.8 us
    ppermute x6, starting transfers between devices, passed_along(): lax.ppermute(value, axis, [(source, source + steps) for source in range(f...  20.6 us
    psum x1, blocking collectives, local(): lax.psum((jnp.sum(q_wide * q_wide, axis=1), jnp.sum(k_wide * k_wide, axis...  2.47 us
  transfers between devices with their start and end apart: 7, of which 1 were waited for; matrix products, arithmetic and copies ran while one was open for 6% of the time, Pallas kernels for 0%

commit v1 on v0

--- a/solution.py
+++ b/solution.py
@@ -18,7 +18,7 @@
 
 def spread(value, axis, source):
     kept = jnp.where(lax.axis_index(axis) == source, value, 0).astype(value.dtype)
-    return lax.psum(kept, axis)
+    return jnp.sum(lax.all_gather(kept, axis), axis=0)
 
 
 def slide_rows(buffer, offset_rows, window_len):

time: 112 us -> 97.8 us (0.87)
  blocking collectives: 2.47 us -> 65.8 us
  waiting for transfers between devices: 60.8 us -> 0.03 us
  between operations: 16.3 us -> 3 us
    all_gather x0 -> x2, blocking collectives: none -> 63.2 us  [spread(): return jnp.sum(lax.all_gather(kept, axis), axis=0)]
    psum x1 -> x0, waiting for transfers between devices: 60.8 us -> none  [spread(): return lax.psum(kept, axis)]
    reshape x2 -> x0, other arithmetic: 1.3 us -> none  [the longest x1 0.65 us: score_block(): k_heads = key_rows.reshape(key_rows.shape[0], head_count, HD)]
  transfers between devices with their start and end apart: 7 -> 6, of which waited for: 1 -> 0; matrix products, arithmetic and copies ran while one was open for 6% -> 3% of each run, Pallas kernels for 0% -> 0%
where the time goes in v1:
time: 97.8 us; the launch traced here: 97.4 us
  blocking collectives  65.8 us (67%)
  starting transfers between devices  19.8 us (20%)
  local copies, waits for them, and re-layouts  3.78 us (4%)
  other arithmetic  3.12 us (3%)
  between operations  3 us (3%)
  matrix products  1.78 us (2%)
    all_gather x2, blocking collectives, spread(): return jnp.sum(lax.all_gather(kept, axis), axis=0)  63.2 us
    ppermute x6, starting transfers between devices, passed_along(): lax.ppermute(value, axis, [(source, source + steps) for source in range(f...  19.8 us
    psum x1, blocking collectives, local(): lax.psum((jnp.sum(q_wide * q_wide, axis=1), jnp.sum(k_wide * k_wide, axis...  2.63 us
  transfers between devices with their start and end apart: 6, of which 0 were waited for; matrix products, arithmetic and copies ran while one was open for 3% of the time, Pallas kernels for 0%

profile of v1, /device:TPU:0, one launch (start us, length us, event | category | flops | bytes accessed | tf_op | source)
XLA Modules:
  0.0 97.4 jit_solution(17234070021574329908)
XLA Ops:
  0.7 1.2 %fusion.10 = f32[96]{0:T(128)S(1)} fusion(bf16[96,1280]{1,0:T(8,128)(2,1)} %param.8), kind=kLoop, calls=%fused_computation.24 | loop fusion | flops 368544 | bytes 246144 | tf_op jit(solution)/shard_map/reduce_sum | solution.py:50
  1.9 0.1 fusion.7
  2.0 2.6 %all-reduce.3 = (f32[96]{0:T(128)S(1)}, f32[96]{0:T(128)S(1)}) all-reduce(f32[96]{0:T(128)S(1)} %fusion.7, f32[96]{0:T(128)S(1)} %fusion.10), channel_id=1, replica_groups=mesh['groups'=2,'tm'=8,'head'=2] {'head'}, use_global_device_ids=true, to_apply=%region_1.0 | all-reduce | flops 192 | bytes 1536 | tf_op jit(solution)/shard_map/psum | solution.py:49
  4.7 0.1 fusion.12
  4.8 0.8 copy-done
  5.6 0.2 fusion.18
  5.8 4.7 %collective-permute-start.2 = (bf16[64,1280]{1,0:T(8,128)(2,1)S(1)}, bf16[64,1280]{1,0:T(8,128)(2,1)S(1)}, u32[]{:S(2)}, u32[]{:S(2)}) collective-permute-start(bf16[64,1280]{1,0:T(8,128)(2,1)S(1)} %get-tuple-element.8), channel_id=1, source_target_pairs={{0,2},{2,4},{4,6},{6,8},{8,10},{10,12},{12,14},{1,3},{3,5},{5,7},{... | collective-permute-start | bytes 491528 | tf_op jit(solution)/shard_map/ppermute | solution.py:16
  10.5 3.5 %collective-permute-start.3 = (bf16[64,1280]{1,0:T(8,128)(2,1)S(1)}, bf16[64,1280]{1,0:T(8,128)(2,1)S(1)}, u32[]{:S(2)}, u32[]{:S(2)}) collective-permute-start(bf16[64,1280]{1,0:T(8,128)(2,1)S(1)} %get-tuple-element.8), channel_id=1, source_target_pairs={{0,4},{2,6},{4,8},{6,10},{8,12},{10,14},{1,5},{3,7},{5,9},{7,11},{... | collective-permute-start | bytes 491528 | tf_op jit(solution)/shard_map/ppermute | solution.py:16
  14.0 3.5 %collective-permute-start.4 = (bf16[64,1280]{1,0:T(8,128)(2,1)S(1)}, bf16[64,1280]{1,0:T(8,128)(2,1)S(1)}, u32[]{:S(2)}, u32[]{:S(2)}) collective-permute-start(bf16[64,1280]{1,0:T(8,128)(2,1)S(1)} %get-tuple-element.7), channel_id=1, source_target_pairs={{0,2},{2,4},{4,6},{6,8},{8,10},{10,12},{12,14},{1,3},{3,5},{5,7},{... | collective-permute-start | bytes 491528 | tf_op jit(solution)/shard_map/ppermute | solution.py:16
  17.5 3.5 %collective-permute-start.5 = (bf16[64,1280]{1,0:T(8,128)(2,1)S(1)}, bf16[64,1280]{1,0:T(8,128)(2,1)S(1)}, u32[]{:S(2)}, u32[]{:S(2)}) collective-permute-start(bf16[64,1280]{1,0:T(8,128)(2,1)S(1)} %get-tuple-element.7), channel_id=1, source_target_pairs={{0,4},{2,6},{4,8},{6,10},{8,12},{10,14},{1,5},{3,7},{5,9},{7,11},{... | collective-permute-start | bytes 491528 | tf_op jit(solution)/shard_map/ppermute | solution.py:16
  21.0 3.4 %collective-permute-start = (bf16[64]{0:T(256)(128)(2,1)S(1)}, bf16[64]{0:T(256)(128)(2,1)S(1)}, u32[]{:S(2)}, u32[]{:S(2)}) collective-permute-start(bf16[64]{0:T(256)(128)(2,1)S(1)} %compare_convert_fusion), channel_id=1, source_target_pairs={{0,2},{2,4},{4,6},{6,8},{8,10},{10,12},{12,14},{1,3},{3,5},{5,7},{... | collective-permute-start | bytes 392 | tf_op jit(solution)/shard_map/ppermute | solution.py:16
  24.4 0.2 copy.17
  24.6 0.2 copy.24
  24.9 0.6 copy-done.5
  25.5 0.6 fusion.29
  26.1 0.1 fusion.9
  26.3 0.2 copy.16
  26.5 31.8 %all-gather = bf16[256,1280]{1,0:T(8,128)(2,1)S(1)} all-gather(bf16[32,1280]{1,0:T(8,128)(2,1)S(1)} %slice_select_fusion), channel_id=2, replica_groups=mesh['groups'=2,'tm'=8,'head'=2] {'tm'}, dimensions={0}, use_global_device_ids=true | all-gather | bytes 737280 | tf_op jit(solution)/shard_map/all_gather | solution.py:21
  59.7 31.4 %all-gather.1 = bf16[256,1280]{1,0:T(8,128)(2,1)S(1)} all-gather(bf16[32,1280]{1,0:T(8,128)(2,1)S(1)} %slice_select_fusion.1), channel_id=3, replica_groups=mesh['groups'=2,'tm'=8,'head'=2] {'tm'}, dimensions={0}, use_global_device_ids=true | all-gather | bytes 737280 | tf_op jit(solution)/shard_map/all_gather | solution.py:21
  91.2 0.3 fusion.31
  91.4 0.2 fusion.30
  91.8 1.3 %collective-permute-start.1 = (bf16[64]{0:T(256)(128)(2,1)S(1)}, bf16[64]{0:T(256)(128)(2,1)S(1)}, u32[]{:S(2)}, u32[]{:S(2)}) collective-permute-start(bf16[64]{0:T(256)(128)(2,1)S(1)} %compare_convert_fusion), channel_id=1, source_target_pairs={{0,4},{2,6},{4,8},{6,10},{8,12},{10,14},{1,5},{3,7},{5,9},{7,11},{... | collective-permute-start | bytes 392 | tf_op jit(solution)/shard_map/ppermute | solution.py:16
  93.1 0.6 convert_reduce_fusion.3
  94.5 0.2 fusion.16
  94.7 0.2 select_reduce_fusion
  94.9 0.2 convert_reduce_fusion.1
  95.1 0.1 convert_reduce_fusion
  95.2 0.4 convolution_bitcast_fusion.2
  95.6 0.4 fusion.1
  96.0 0.3 fusion.5
  96.3 0.2 copy.29
  96.5 0.9 copy.30
  (29 shorter events, 0.4 us)
Async XLA Ops:
  0.0 1.9 %copy-start.2 = (bf16[96,1280]{1,0:T(8,128)(2,1)S(1)}, bf16[96,1280]{1,0:T(8,128)(2,1)}, u32[]{:S(2)}) copy-start(bf16[96,1280]{1,0:T(8,128)(2,1)} %param.7) | copy-start | bytes 737284
  0.7 4.0 %copy-start.1 = (bf16[96,1280]{1,0:T(8,128)(2,1)S(1)}, bf16[96,1280]{1,0:T(8,128)(2,1)}, u32[]{:S(2)}) copy-start(bf16[96,1280]{1,0:T(8,128)(2,1)} %param.8) | copy-start | bytes 737284
  2.0 2.7 %copy-start.3 = (f32[1280]{0:T(1024)S(1)}, f32[1280]{0:T(1024)}, u32[]{:S(2)}) copy-start(f32[1280]{0:T(1024)} %param.11) | copy-start | bytes 15364
  4.7 0.9 copy-start
  5.8 88.6 %collective-permute-start.2 = (bf16[64,1280]{1,0:T(8,128)(2,1)S(1)}, bf16[64,1280]{1,0:T(8,128)(2,1)S(1)}, u32[]{:S(2)}, u32[]{:S(2)}) collective-permute-start(bf16[64,1280]{1,0:T(8,128)(2,1)S(1)} %get-tuple-element.8), channel_id=1, source_target_pairs={{0,2},{2,4},{4,6},{6,8},{8,10},{10,12},{12,14},{1,3},{3,5},{5,7},{... | collective-permute-start | bytes 491528 | tf_op jit(solution)/shard_map/ppermute | solution.py:16
  10.5 83.9 %collective-permute-start.3 = (bf16[64,1280]{1,0:T(8,128)(2,1)S(1)}, bf16[64,1280]{1,0:T(8,128)(2,1)S(1)}, u32[]{:S(2)}, u32[]{:S(2)}) collective-permute-start(bf16[64,1280]{1,0:T(8,128)(2,1)S(1)} %get-tuple-element.8), channel_id=1, source_target_pairs={{0,4},{2,6},{4,8},{6,10},{8,12},{10,14},{1,5},{3,7},{5,9},{7,11},{... | collective-permute-start | bytes 491528 | tf_op jit(solution)/shard_map/ppermute | solution.py:16
  14.0 80.4 %collective-permute-start.4 = (bf16[64,1280]{1,0:T(8,128)(2,1)S(1)}, bf16[64,1280]{1,0:T(8,128)(2,1)S(1)}, u32[]{:S(2)}, u32[]{:S(2)}) collective-permute-start(bf16[64,1280]{1,0:T(8,128)(2,1)S(1)} %get-tuple-element.7), channel_id=1, source_target_pairs={{0,2},{2,4},{4,6},{6,8},{8,10},{10,12},{12,14},{1,3},{3,5},{5,7},{... | collective-permute-start | bytes 491528 | tf_op jit(solution)/shard_map/ppermute | solution.py:16
  17.5 77.0 %collective-permute-start.5 = (bf16[64,1280]{1,0:T(8,128)(2,1)S(1)}, bf16[64,1280]{1,0:T(8,128)(2,1)S(1)}, u32[]{:S(2)}, u32[]{:S(2)}) collective-permute-start(bf16[64,1280]{1,0:T(8,128)(2,1)S(1)} %get-tuple-element.7), channel_id=1, source_target_pairs={{0,4},{2,6},{4,8},{6,10},{8,12},{10,14},{1,5},{3,7},{5,9},{7,11},{... | collective-permute-start | bytes 491528 | tf_op jit(solution)/shard_map/ppermute | solution.py:16
  21.0 70.8 %collective-permute-start = (bf16[64]{0:T(256)(128)(2,1)S(1)}, bf16[64]{0:T(256)(128)(2,1)S(1)}, u32[]{:S(2)}, u32[]{:S(2)}) collective-permute-start(bf16[64]{0:T(256)(128)(2,1)S(1)} %compare_convert_fusion), channel_id=1, source_target_pairs={{0,2},{2,4},{4,6},{6,8},{8,10},{10,12},{12,14},{1,3},{3,5},{5,7},{... | collective-permute-start | bytes 392 | tf_op jit(solution)/shard_map/ppermute | solution.py:16
  24.9 0.7 copy-start.5
  24.9 1.2 %copy-start.4 = (f32[1280]{0:T(1024)S(1)}, f32[1280]{0:T(1024)}, u32[]{:S(2)}) copy-start(f32[1280]{0:T(1024)} %param.10) | copy-start | bytes 15364
  91.8 2.6 %collective-permute-start.1 = (bf16[64]{0:T(256)(128)(2,1)S(1)}, bf16[64]{0:T(256)(128)(2,1)S(1)}, u32[]{:S(2)}, u32[]{:S(2)}) collective-permute-start(bf16[64]{0:T(256)(128)(2,1)S(1)} %compare_convert_fusion), channel_id=1, source_target_pairs={{0,4},{2,6},{4,8},{6,10},{8,12},{10,14},{1,5},{3,7},{5,9},{7,11},{... | collective-permute-start | bytes 392 | tf_op jit(solution)/shard_map/ppermute | solution.py:16
